TPU v7x, 512 devices: a whole 4x8x8 slice. The times are simulated.
512 devices in a mesh: seq: 64 (over y, z), tp: 8 (over x, core).
Axes of the slice: x: 4, y: 8, z: 8, core: 2. Of those that a mesh axis runs over, the one named last changes fastest.
Arguments:
- queries: bfloat16 [16384, 8192], P('seq', 'tp'), may hold values from -12 to 12
- kv_rows: bfloat16 [16384, 2048], P('seq', 'tp'), may hold values from -6 to 6
- vertical: int32 [64, 32], replicated, may hold values from 0 to 255, as said below
- slash: int32 [64, 8], replicated, may hold values from 0 to 11, as said below
Outputs:
- attended: bfloat16 [16384, 8192], P(('seq', 'tp'))
Inputs may be any that keep to these rules, and one draw needn't show every extreme that they name: `vertical`: each row lists 32 distinct blocks in rising order and includes block 0 and block 255. The heads that share one key-value head list together exactly 48 distinct blocks. `slash`: each row lists 8 distinct offsets in rising order, the first 0 and the last 11.
All inputs are finite; a program needn't handle non-finite values.
Results may differ from a plain program's by a relative error of at most 0.0045.
Values may be sent and summed in bfloat16 or wider, within the bound.
A program may use at most 64 MiB of HBM per device.

v0:
```python
import jax
import jax.numpy as jnp
from jax import lax
from jax.sharding import PartitionSpec as P

HEAD_SIZE = 128
BLK = 64


def as_sent(array):

    def short(part):
        return part.astype(jnp.bfloat16) if part.dtype == jnp.float32 else part

    return jax.tree.map(short, array)


def key_mask(bids, vertical_row, srow):
    dist = bids[:, None] - vertical_row[None, :]
    hit = jnp.any(dist[:, :, None] == srow[None, None, :], axis=2)
    live_v = jnp.logical_and(dist >= 0, jnp.logical_not(hit))
    live_s = bids[:, None] - srow[None, :] >= 0
    live = jnp.concatenate([live_v, live_s], axis=1)
    diag = jnp.concatenate([jnp.zeros(vertical_row.shape, bool), srow == 0])
    rows = jnp.arange(BLK, dtype=jnp.int32)
    lower = rows[None, :] <= rows[:, None]
    return live[:, None, :, None] & (
        jnp.logical_not(diag)[None, None, :, None] | lower[None, :, None, :]
    )


def attend(query_block, vert_block, slash_block, bids, vertical_row, srow):
    count_v = vert_block.shape[0]
    scale = 1.0 / HEAD_SIZE**0.5
    logit_vert = jnp.einsum(
        "unz,syz->unsy",
        query_block,
        vert_block[..., :HEAD_SIZE],
        preferred_element_type=jnp.float32,
    )
    logit_slash = jnp.einsum(
        "unz,suyz->unsy",
        query_block,
        slash_block[..., :HEAD_SIZE],
        preferred_element_type=jnp.float32,
    )
    logit_matrix = jnp.concatenate([logit_vert, logit_slash], axis=2) * scale
    mask = key_mask(bids, vertical_row, srow)
    logit_matrix = jnp.where(mask, logit_matrix, -1e30)
    top = jnp.max(logit_matrix, axis=(2, 3), keepdims=True)
    weights = jnp.where(mask, jnp.exp(logit_matrix - top), 0.0)
    total = jnp.sum(weights, axis=(2, 3))
    probabilities = weights.astype(jnp.bfloat16)
    weighted_sum = jnp.einsum(
        "unsy,syd->und",
        probabilities[:, :, :count_v],
        vert_block[..., HEAD_SIZE:],
        preferred_element_type=jnp.float32,
    )
    weighted_sum = weighted_sum + jnp.einsum(
        "unsy,suyd->und",
        probabilities[:, :, count_v:],
        slash_block[..., HEAD_SIZE:],
        preferred_element_type=jnp.float32,
    )
    return (weighted_sum / total[..., None]).astype(jnp.bfloat16)


def slash_slices(table, starts, key_value_head, block_list):
    pieces = []
    for index in range(starts.shape[0]):
        piece = lax.dynamic_slice(
            table,
            (starts[index], 0, key_value_head, 0),
            (block_list, table.shape[1], 1, table.shape[3]),
        )
        pieces.append(piece[:, :, 0])
    return jnp.stack(pieces, axis=0)


def per_device(queries, kv_rows, vertical, slash):
    tok = queries.shape[0]
    n_tp = lax.axis_size("tp")
    heads_loc = vertical.shape[0] // n_tp
    kv_loc = kv_rows.shape[1] // (2 * HEAD_SIZE)
    group = heads_loc // kv_loc
    block_list = tok // BLK
    seq_pos = lax.axis_index("seq")
    tp_pos = lax.axis_index("tp")
    my_vert = lax.dynamic_slice_in_dim(vertical, tp_pos * heads_loc, heads_loc, 0)
    my_slash = lax.dynamic_slice_in_dim(slash, tp_pos * heads_loc, heads_loc, 0)
    first = seq_pos * block_list
    bids = first + jnp.arange(block_list, dtype=jnp.int32)
    full = lax.all_gather(kv_rows, "seq", axis=0, tiled=True)
    index_table = full.reshape(full.shape[0] // BLK, BLK, kv_loc, 2 * HEAD_SIZE)
    front = 3 * block_list
    padded = jnp.concatenate(
        [jnp.zeros((front, BLK, kv_loc, 2 * HEAD_SIZE), index_table.dtype), index_table], axis=0
    )

    def gather_rows(key_value_head, vertical_row, srow):
        vert_block = index_table[vertical_row, :, key_value_head]
        starts = first + front - srow
        return (vert_block, slash_slices(padded, starts, key_value_head, block_list))

    qheads = jnp.transpose(queries.reshape(block_list, BLK, heads_loc, HEAD_SIZE), (2, 0, 1, 3))

    def one_head(item):
        query_block, vertical_row, srow, key_value_head = item
        vert_block, slash_block = gather_rows(key_value_head, vertical_row, srow)
        return attend(query_block, vert_block, slash_block, bids, vertical_row, srow)

    owners = jnp.arange(heads_loc, dtype=jnp.int32) // group
    outputs = lax.map(one_head, (qheads, my_vert, my_slash, owners))
    attn = jnp.transpose(outputs, (1, 2, 0, 3)).reshape(tok, heads_loc * HEAD_SIZE)
    return lax.all_to_all(as_sent(attn), "tp", split_axis=0, concat_axis=1, tiled=True).astype(
        attn.dtype
    )


def solution(mesh):
    return jax.shard_map(
        per_device,
        mesh=mesh,
        in_specs=(P("seq", "tp"), P("seq", "tp"), P(), P()),
        out_specs=P(("seq", "tp"), None),
        check_vma=False,
    )
```

profile of v0, /device:TPU:1, one launch (start us, length us, event | category | flops | bytes accessed | tf_op | source)
XLA Modules:
  0.0 460.2 jit_solution(17042066455035108971)
XLA Ops:
  10.4 104.9 %all-gather.2.cloned.1.call-done = bf16[16384,256]{1,0:T(8,128)(2,1)} async-done(((bf16[256,256]{1,0:T(8,128)(2,1)}), bf16[16384,256]{1,0:T(8,128)(2,1)}) %all-gather.2.cloned.1.call-update) | async-done | bytes 8388624 | tf_op jit(solution)/shard_map/all_gather | solution.py:94
  115.2 8.4 %concatenate.19 = bf16[268,64,1,256]{3,1,0,2:T(8,128)(2,1)} pad(bf16[256,64,1,256]{3,1,0,2:T(8,128)(2,1)} %bitcast.144, bf16[]{:T(256)} %constant.98.clone.1), padding=12_0x0_0x0_0x0_0 | pad | bytes 17170434 | tf_op jit(solution)/shard_map/concatenate | solution.py:97
  123.7 313.1 %while.13 = (s32[]{:T(128)}, bf16[8,4,64,128]{3,2,1,0:T(8,128)(2,1)}, s32[8,32]{1,0:T(8,128)S(1)}, s32[8,8]{1,0:T(8,128)S(1)}, bf16[8,4,64,128]{3,2,1,0:T(8,128)...) while((s32[]{:T(128)}, ...), condition=%wide.region_4.5_spmd.clone, body=%wide.region_0.4_spmd.clone.sunk | while | flops 344332768 | bytes 21678552 | solution.py:114
  150.7 4.0 gather_fusion
  154.7 1.6 fusion.53
  156.6 1.4 fusion.55
  158.1 3.0 fusion.56
  189.9 4.0 gather_fusion
  193.9 1.6 fusion.53
  195.8 1.4 fusion.55
  197.2 3.0 fusion.56
  229.0 4.0 gather_fusion
  233.0 1.6 fusion.53
  234.9 1.4 fusion.55
  236.3 3.0 fusion.56
  268.1 4.0 gather_fusion
  272.1 1.6 fusion.53
  274.0 1.4 fusion.55
  275.5 3.0 fusion.56
  307.3 4.0 gather_fusion
  311.3 1.6 fusion.53
  314.6 3.0 fusion.56
  346.4 4.0 gather_fusion
  350.4 1.6 fusion.53
  353.7 3.0 fusion.56
  385.5 4.0 gather_fusion
  389.6 1.6 fusion.53
  392.9 3.0 fusion.56
  424.7 4.0 gather_fusion
  428.7 1.6 fusion.53
  432.0 3.0 fusion.56
  438.4 14.1 %all_to_all.19 = bf16[8,32,1024]{2,1,0:T(8,128)(2,1)S(1)} all-to-all(bf16[8,32,1024]{2,1,0:T(8,128)(2,1)S(1)} %all_to_all.14), channel_id=1, replica_groups=mesh['seq'=64,'tp'=8] {'tp'}, dimensions={0} | all-to-all | bytes 1048576 | tf_op jit(solution)/shard_map/all_to_all | solution.py:116
  (228 shorter events, 109.5 us)
Async XLA Ops:
  6.5 0.7 copy-start
  6.5 108.7 %all-gather.2.cloned.1.call-start = ((), (), s32[]{:S(2)}) async-start(), calls=%async_computation.1 | async-start | bytes 8519680 | tf_op jit(solution)/shard_map/all_gather | solution.py:94
Sparse Core Ops, SparseCore 0:
  10.4 104.8 all-gather.1
where the time goes:
time: 465 us; the launch traced here: 460 us
  loops' own time  135 us (29%)
  local copies, waits for them, and re-layouts  115 us (25%)
  waiting for transfers between devices  106 us (23%)
  other arithmetic  41.5 us (9%)
  matrix products  35.1 us (8%)
  blocking collectives  14.1 us (3%)
  between operations  13.4 us (3%)
    another operation x1, loops' own time, per_device(): outputs = lax.map(one_head, (qheads, my_vert, my_slash, owners))  135 us
    all_gather x1, waiting for transfers between devices, per_device(): full = lax.all_gather(kv_rows, 'seq', axis=0, tiled=True)  105 us
    while x56, local copies, waits for them, and re-layouts  51.4 us
    gather x8, local copies, waits for them, and re-layouts, gather_rows(): vert_block = index_table[vertical_row, :, key_value_head]  32 us
    reduce_sum x8, other arithmetic, attend(): total = jnp.sum(weights, axis=(2, 3))  24.2 us
    all_to_all x1, blocking collectives, per_device(): lax.all_to_all(as_sent(attn), 'tp', split_axis=0, concat_axis=1, tiled=True)  14.1 us
    dot_general x8, matrix products, attend(): jnp.einsum('unz,syz->unsy', query_block, vert_block[..., :HEAD_SIZE], pre...  12.5 us
    reduce_max x8, other arithmetic, attend(): top = jnp.max(logit_matrix, axis=(2, 3), keepdims=True)  11.5 us
  transfers between devices with their start and end apart: 1, of which 1 were waited for; matrix products, arithmetic and copies ran while one was open for 1% of the time, Pallas kernels for 0%

commit v1 on v0

v1 whole, which is shorter than its diff:
```python
import jax
import jax.numpy as jnp
from jax import lax
from jax.experimental import pallas as pl
from jax.experimental.pallas import tpu as pltpu
from jax.sharding import PartitionSpec as P

HEAD_SIZE = 128
BLK = 64
SIDE = 8
NPIECE = 8
GV = 48
HEADS_LOC = 8
NTP = 8
MASKED = -1e30
MESH = pl.DeviceIdType.MESH
LOG2E = 1.4426950408889634


def kv_kernel(sel_ref, kv_ref, pk_ref, pv_ref, wk_ref, wv_ref, p2k, p2v,
              a2a_send, a2a_recv, ring2_send, ring2_recv, ring3_send, ring3_recv,
              win_send, win_recv, loc_sem):
    seq = lax.axis_index("seq")
    y, z = seq // SIDE, seq % SIDE

    def at(yy, zz):
        return {"seq": (yy % SIDE) * SIDE + zz % SIDE}

    nxt = {"seq": (seq + 1) % (SIDE * SIDE)}
    prv = {"seq": (seq + SIDE * SIDE - 1) % (SIDE * SIDE)}

    barrier = pltpu.get_barrier_semaphore()
    for j in range(1, SIDE):
        pl.semaphore_signal(barrier, inc=1, device_id=at(y + j, z), device_id_type=MESH)
        pl.semaphore_signal(barrier, inc=1, device_id=at(y, z + j), device_id_type=MESH)
    pl.semaphore_signal(barrier, inc=1, device_id=nxt, device_id_type=MESH)
    pl.semaphore_signal(barrier, inc=1, device_id=prv, device_id_type=MESH)

    own = [
        pltpu.make_async_copy(kv_ref.at[:, y, :, 0:128], p2k.at[z, y], loc_sem.at[0]),
        pltpu.make_async_copy(kv_ref.at[:, z, :, 128:256], p2v.at[y, z], loc_sem.at[1]),
        pltpu.make_async_copy(kv_ref.at[:, :, :, 0:128], wk_ref.at[3], loc_sem.at[2]),
        pltpu.make_async_copy(kv_ref.at[:, :, :, 128:256], wv_ref.at[3], loc_sem.at[3]),
    ]
    for copy in own:
        copy.start()
    pl.semaphore_wait(barrier, 2 * (SIDE - 1) + 2)

    sends = []

    def remote(src, dst, ssem, rsem, dev):
        copy = pltpu.make_async_remote_copy(
            src_ref=src, dst_ref=dst, send_sem=ssem, recv_sem=rsem, device_id=dev,
            device_id_type=MESH)
        copy.start()
        sends.append(copy)
        return copy

    first = []
    for j in (4, 3, 5, 2, 6, 1, 7):
        p = (y + j) % SIDE
        first.append(remote(kv_ref.at[:, p, :, 0:128], p2k.at[z, y],
                            a2a_send.at[0, j - 1], a2a_recv.at[0, j - 1], at(y + j, z)))
        q = (z + j) % SIDE
        first.append(remote(kv_ref.at[:, q, :, 128:256], p2v.at[y, z],
                            a2a_send.at[1, j - 1], a2a_recv.at[1, j - 1], at(y, z + j)))
    for copy in own:
        copy.wait()
    window = []
    for half, ref in ((0, wk_ref), (1, wv_ref)):
        window.append(remote(ref.at[3], ref.at[2], win_send.at[half, 0], win_recv.at[half, 0], nxt))
    for copy in first:
        copy.wait_recv()

    def ring(bufs, sems_s, sems_r, middle):
        def send(index, sign, k):
            buf, c, dev = bufs[index]
            src = (c - sign * (k - 1)) % SIDE
            d = 0 if sign > 0 else 1
            return remote(buf.at[src], buf.at[src], sems_s.at[index, d, k - 1],
                          sems_r.at[index, d, k - 1], dev(sign))

        live = {}
        for index in (0, 1):
            for sign in (1, -1):
                live[index, sign] = send(index, sign, 1)
        for k in range(1, 5):
            for index in (0, 1):
                for sign in (-1, 1):
                    if (index, sign) in live:
                        live[index, sign].wait_recv()
                        if k < (3 if sign > 0 else 4):
                            live[index, sign] = send(index, sign, k + 1)
                        else:
                            del live[index, sign]
            middle(k)

    def forward_window(k):
        if k in (1, 2):
            for half, ref in ((0, wk_ref), (1, wv_ref)):
                window[-2].wait_recv()
                window.append(remote(ref.at[3 - k], ref.at[2 - k], win_send.at[half, k],
                                     win_recv.at[half, k], nxt))

    along_y = lambda sign: at(y + SIDE + sign, z)
    along_z = lambda sign: at(y, z + SIDE + sign)
    ring([(p2k, z, along_z), (p2v, y, along_y)], ring2_send, ring2_recv, forward_window)

    @pl.loop(0, GV)
    def _(s):
        b = sel_ref[s]
        by, bz, bi = b // (4 * SIDE), (b // 4) % SIDE, b % 4
        pk_ref[y, s] = p2k[bz, by, bi]
        pv_ref[z, s] = p2v[by, bz, bi]

    ring([(pk_ref, y, along_y), (pv_ref, z, along_z)], ring3_send, ring3_recv, lambda k: None)
    for copy in window[-2:]:
        copy.wait_recv()
    for copy in sends:
        copy.wait_send()


def attend_kernel(q_ref, bias_ref, k_ref, v_ref, wk_ref, wv_ref, out_ref, attn, send, recv, loc_sem):
    seq = lax.axis_index("seq")
    tp = lax.axis_index("tp")
    barrier = pltpu.get_barrier_semaphore()
    for j in range(1, NTP):
        pl.semaphore_signal(barrier, inc=1, device_id={"tp": (tp + j) % NTP}, device_id_type=MESH)
    pl.semaphore_wait(barrier, NTP - 1)
    scale = LOG2E / HEAD_SIZE**0.5
    rows = attn.shape[1]
    own = 4 * BLK
    chunk = 768

    def pattern(shape, value):
        lane = lax.broadcasted_iota(jnp.int32, shape, 1)
        row = lax.broadcasted_iota(jnp.int32, shape, 0)
        return jnp.where(lane == value(row), 1.0, 0.0).astype(jnp.bfloat16)

    def contract(a, b):
        return lax.dot_general(a, b, (((1,), (1,)), ((), ())), preferred_element_type=jnp.float32)

    def one_head(h, carry):
        lanes = pl.ds(pl.multiple_of(h * HEAD_SIZE, HEAD_SIZE), HEAD_SIZE)
        q = q_ref[:, lanes]
        bias = bias_ref[h]
        qbias = jnp.concatenate(
            [jnp.broadcast_to(bias[b:b + 1], (BLK, HEAD_SIZE)) for b in range(4)], axis=0)
        qa = jnp.concatenate([q, qbias.astype(jnp.bfloat16)], axis=1)
        ones = jnp.ones((4 * own, HEAD_SIZE), jnp.bfloat16)

        wk = wk_ref[...]
        ka = jnp.concatenate([wk, pattern((4 * own, HEAD_SIZE), lambda r: GV + r // BLK)], axis=1)
        s = contract(qa, ka)
        qrow = lax.broadcasted_iota(jnp.int32, (own, own), 0)
        kcol = lax.broadcasted_iota(jnp.int32, (own, own), 1)
        s = jnp.concatenate([s[:, :3 * own], jnp.where(kcol > qrow, MASKED, s[:, 3 * own:])], axis=1)
        m = jnp.max(s, axis=1, keepdims=True)
        p = jnp.exp2((s - m) * scale).astype(jnp.bfloat16)
        acc = jnp.dot(p, jnp.concatenate([wv_ref[...], ones], axis=1), preferred_element_type=jnp.float32)
        for c in range(NPIECE * GV * 8 // chunk):
            k = k_ref[c * chunk:(c + 1) * chunk]
            v = v_ref[c * chunk:(c + 1) * chunk]
            ka = jnp.concatenate([k, pattern((chunk, HEAD_SIZE), lambda r: (r // 8) % GV)], axis=1)
            s = contract(qa, ka)
            m_new = jnp.maximum(m, jnp.max(s, axis=1, keepdims=True))
            alpha = jnp.exp2((m - m_new) * scale)
            p = jnp.exp2((s - m_new) * scale).astype(jnp.bfloat16)
            acc = acc * alpha + jnp.dot(p, jnp.concatenate([v, ones[:chunk]], axis=1),
                                        preferred_element_type=jnp.float32)
            m = m_new
        attn[:, :, lanes] = (acc[:, :HEAD_SIZE] / acc[:, HEAD_SIZE:]).astype(jnp.bfloat16).reshape(
            NTP, rows, HEAD_SIZE)
        for j in range(1, NTP):
            t = (tp + j) % NTP
            pltpu.make_async_remote_copy(
                src_ref=attn.at[t, :, lanes],
                dst_ref=out_ref.at[tp, :, lanes],
                send_sem=send.at[j - 1], recv_sem=recv.at[j - 1],
                device_id={"tp": t}, device_id_type=MESH).start()
        return carry

    lax.fori_loop(0, HEADS_LOC, one_head, 0)
    mine = pltpu.make_async_copy(attn.at[tp], out_ref.at[tp], loc_sem)
    mine.start()
    mine.wait()
    for j in range(1, NTP):
        t = (tp + j) % NTP
        copy = pltpu.make_async_remote_copy(
            src_ref=attn.at[t], dst_ref=out_ref.at[tp], send_sem=send.at[j - 1],
            recv_sem=recv.at[j - 1], device_id={"tp": t}, device_id_type=MESH)
        copy.wait_send()
        copy.wait_recv()


def tables(vert, srow, first):
    ids = jnp.arange(256, dtype=jnp.int32)
    present = jnp.any(vert.reshape(-1, 1) == ids[None, :], axis=0)
    rank = jnp.sum((present[None, :] & (ids[None, :] <= ids[:, None])).astype(jnp.int32), axis=1)
    slot = jnp.arange(GV, dtype=jnp.int32)
    sel = jnp.sum(jnp.where(present[None, :] & (rank[None, :] == slot[:, None] + 1), ids[None, :], 0), axis=1)
    bids = first + jnp.arange(4, dtype=jnp.int32)
    listed = jnp.any(vert[:, None, :] == sel[None, :, None], axis=2)
    dist = bids[:, None] - sel[None, :]
    hit = jnp.any(dist[None, :, :, None] == srow[:, None, None, :], axis=3)
    live_v = listed[:, None, :] & (dist >= 0)[None] & jnp.logical_not(hit)
    w = jnp.arange(16, dtype=jnp.int32)
    offset = jnp.arange(4, dtype=jnp.int32)[:, None] + 12 - w[None, :]
    live_w = jnp.any(offset[None, :, :, None] == srow[:, None, None, :], axis=3)
    live_w = live_w & (first - 12 + w >= 0)[None, None, :]
    live = jnp.concatenate([live_v, live_w], axis=2)
    bias = jnp.where(live, 0.0, MASKED).astype(jnp.float32)
    return sel, jnp.concatenate([bias, jnp.zeros_like(bias)], axis=2)


def per_device(queries, kv_rows, vertical, slash):
    tok = queries.shape[0]
    seq_pos = lax.axis_index("seq")
    tp_pos = lax.axis_index("tp")
    vert = lax.dynamic_slice_in_dim(vertical, tp_pos * HEADS_LOC, HEADS_LOC, 0)
    srow = lax.dynamic_slice_in_dim(slash, tp_pos * HEADS_LOC, HEADS_LOC, 0)
    sel, bias = tables(vert, srow, seq_pos * 4)
    vmem = pl.BlockSpec(memory_space=pltpu.VMEM)
    dma = pltpu.SemaphoreType.DMA
    pk, pv, wk, wv = pl.pallas_call(
        kv_kernel,
        out_shape=[jax.ShapeDtypeStruct((NPIECE, GV, 8, 128), jnp.bfloat16)] * 2
        + [jax.ShapeDtypeStruct((4, 4, 8, 8, 128), jnp.bfloat16)] * 2,
        in_specs=[pl.BlockSpec(memory_space=pltpu.SMEM), vmem],
        out_specs=[vmem] * 4,
        scratch_shapes=[
            pltpu.VMEM((SIDE, SIDE, 4, 8, 128), jnp.bfloat16),
            pltpu.VMEM((SIDE, SIDE, 4, 8, 128), jnp.bfloat16),
            dma((2, 7)), dma((2, 7)), dma((2, 2, 4)), dma((2, 2, 4)), dma((2, 2, 4)), dma((2, 2, 4)),
            dma((2, 3)), dma((2, 3)), dma((4,)),
        ],
        compiler_params=pltpu.CompilerParams(collective_id=0, has_side_effects=True),
        name="kv_exchange",
    )(sel, kv_rows.reshape(4, NPIECE, 8, 256))
    rows = tok // NTP
    out = pl.pallas_call(
        attend_kernel,
        out_shape=jax.ShapeDtypeStruct((NTP, rows, HEADS_LOC * HEAD_SIZE), jnp.bfloat16),
        in_specs=[vmem] * 6,
        out_specs=vmem,
        scratch_shapes=[
            pltpu.VMEM((NTP, rows, HEADS_LOC * HEAD_SIZE), jnp.bfloat16),
            dma((7,)), dma((7,)), dma(()),
        ],
        compiler_params=pltpu.CompilerParams(collective_id=1, has_side_effects=True),
        name="attend",
    )(queries, bias, pk.reshape(-1, 128), pv.reshape(-1, 128), wk.reshape(-1, 128), wv.reshape(-1, 128))
    return jnp.transpose(out, (1, 0, 2)).reshape(rows, NTP * HEADS_LOC * HEAD_SIZE)


def solution(mesh):
    return jax.shard_map(
        per_device,
        mesh=mesh,
        in_specs=(P("seq", "tp"), P("seq", "tp"), P(), P()),
        out_specs=P(("seq", "tp"), None),
        check_vma=False,
    )
```

time: 465 us -> 87 us (0.19)
  loops' own time: 135 us -> 0 us
  local copies, waits for them, and re-layouts: 115 us -> 3.8 us
  waiting for transfers between devices: 106 us -> 0 us
  Pallas kernels: 0 us -> 81.6 us
  other arithmetic: 41.5 us -> 1.16 us
  matrix products: 35.1 us -> 0 us
  blocking collectives: 14.1 us -> 0 us
  between operations: 13.4 us -> 0.09 us
    another operation x1 -> x0, loops' own time: 135 us -> none  [per_device(): outputs = lax.map(one_head, (qheads, my_vert, my_slash, owners))]
    all_gather x1 -> x0, waiting for transfers between devices: 105 us -> none  [per_device(): full = lax.all_gather(kv_rows, 'seq', axis=0, tiled=True)]
    pallas_call x0 -> x2, Pallas kernels: none -> 81.6 us  [the longest x1 49.6 us: per_device(): pl.pallas_call(kv_kernel, out_shape=[jax.ShapeDtypeStruct((NPIECE, GV, 8,...]
    while x56 -> x0, local copies, waits for them, and re-layouts: 51.4 us -> none
    dot_general x32 -> x0, matrix products: 35.1 us -> none  [the longest x8 12.5 us: attend(): jnp.einsum('unz,syz->unsy', query_block, vert_block[..., :HEAD_SIZE], pre...]
    gather x8 -> x0, local copies, waits for them, and re-layouts: 32 us -> none  [gather_rows(): vert_block = index_table[vertical_row, :, key_value_head]]
    reduce_sum x8 -> x2, other arithmetic: 24.2 us -> 0.3 us  [the longest x1 0.18 us: tables(): jnp.sum(jnp.where(present[None, :] & (rank[None, :] == slot[:, None] + 1)...]
    all_to_all x1 -> x0, blocking collectives: 14.1 us -> none  [per_device(): lax.all_to_all(as_sent(attn), 'tp', split_axis=0, concat_axis=1, tiled=True)]
  transfers between devices with their start and end apart: 1 -> 0, of which waited for: 1 -> 0; matrix products, arithmetic and copies ran while one was open for 1% -> 0% of each run, Pallas kernels for 0% -> 0%
where the time goes in v1:
time: 87 us; the launch traced here: 86.7 us
  Pallas kernels  81.6 us (94%)
  local copies, waits for them, and re-layouts  3.8 us (4%)
  other arithmetic  1.16 us (1%)
    pallas_call x1, Pallas kernels, per_device(): pl.pallas_call(kv_kernel, out_shape=[jax.ShapeDtypeStruct((NPIECE, GV, 8,...  49.6 us
    pallas_call x1, Pallas kernels, per_device(): pl.pallas_call(attend_kernel, out_shape=jax.ShapeDtypeStruct((NTP, rows,...  32 us
    reshape x1, local copies, waits for them, and re-layouts, per_device(): jnp.transpose(out, (1, 0, 2)).reshape(rows, NTP * HEADS_LOC * HEAD_SIZE)  1.88 us

profile of v1, /device:TPU:1, one launch (start us, length us, event | category | flops | bytes accessed | tf_op | source)
XLA Modules:
  0.0 86.7 jit_solution(3767904999628227242)
XLA Ops:
  0.0 0.0 copy-start
  0.0 0.0 copy-start.2
  0.1 0.1 iota_subtract_fusion
  0.1 0.6 copy-done.2
  0.7 0.1 constant_dynamic-slice_fusion
  0.8 0.1 copy.15
  0.9 0.1 compare_reduce_fusion
  1.0 0.0 copy-done
  1.0 0.1 constant_dynamic-slice_fusion.1
  1.1 0.1 copy.13
  1.2 0.1 eq.70
  1.3 0.1 fusion
  1.4 0.1 convert_reduce_fusion
  1.5 0.2 select_reduce_fusion.sel_ref
  1.7 0.0 copy-start.1
  1.7 0.1 compare_reduce_fusion.2
  1.8 0.1 broadcast_compare_fusion
  1.9 0.3 copy-done.1
  2.2 0.1 broadcast_subtract_fusion
  2.3 0.1 compare_reduce_fusion.1
  2.5 0.1 add_select_fusion
  2.5 0.6 concatenate.7.bias_ref
  3.2 49.6 %kv_exchange.1 = (bf16[8,48,8,128]{3,2,1,0:T(8,128)(2,1)}, bf16[8,48,8,128]{3,2,1,0:T(8,128)(2,1)}, bf16[4,4,8,8,128]{4,3,2,1,0:T(8,128)(2,1)}, bf16[4,4,8,8,128]{4,3,2,1,0:T(8,128)(2,1)}) custom-call(s32[48]{0:T(128)} %copy-done.1, bf16[4,8,8,256]{3,2,1,0:T(8,128)(2,1)} %bitcast.13), custom_call_target="tpu_custom_call" | custom-call | tf_op jit(solution)/shard_map/kv_exchange/pallas_call | solution.py:225
  52.8 32.0 %attend.1 = bf16[8,32,1024]{2,1,0:T(8,128)(2,1)} custom-call(bf16[256,1024]{1,0:T(8,128)(2,1)} %q_ref.1, f32[8,4,128]{2,1,0:T(4,128)} %concatenate.7.bias_ref, bf16[3072,128]{1,0:T(8,128)(2,1)} %bitcast.9, bf16[3072,128]{1,0:T(8,128)(2,1)} %bitcast.10, bf16[1024,128]{1,0:T(8,128)(2,1)} %bitcast.11, bf16[1024,128]{1,0:T(8,128)(2,1)} %bitcast.12), custom_call_target="tpu_custom_call" | custom-call | tf_op jit(solution)/shard_map/attend/pallas_call | solution.py:241
  84.8 1.9 %copy.18 = bf16[8,4,8,1024]{3,2,0,1:T(8,128)(2,1)} copy(bf16[8,4,8,1024]{3,2,1,0:T(8,128)(2,1)} %bitcast.8) | data formatting | bytes 1048576 | tf_op jit(solution)/shard_map/reshape | solution.py:253
  (6 shorter events, 0.0 us)
Async XLA Ops:
  0.0 1.0 %copy-start = (s32[64,32]{0,1:T(8,128)S(1)}, s32[64,32]{0,1:T(8,128)}, u32[]{:S(2)}) copy-start(s32[64,32]{0,1:T(8,128)} %param.6) | copy-start | bytes 24580
  0.0 0.7 copy-start.2
  1.7 0.5 copy-start.1
